TPU v7x, 32 devices: a whole 2x2x4 slice. The times are simulated.
32 devices in a mesh: grp: 2 (over x), wide: 16 (over z, y, core).
Axes of the slice: x: 2, y: 2, z: 4, core: 2. Of those that a mesh axis runs over, the one named last changes fastest.
Arguments:
- queries: bfloat16 [256, 4096], P(('grp', 'wide')), parts along dimension 0, may hold values from -8 to 8
- draft_keys: bfloat16 [256, 512], P(('grp', 'wide')), parts along dimension 0, may hold values from -8 to 8
- draft_values: bfloat16 [256, 512], P(('grp', 'wide')), parts along dimension 0, may hold values from -24 to 24
- cache_keys: bfloat16 [262144, 128], P(('grp', 'wide')), parts along dimension 0, may hold values from -8 to 8
- cache_values: bfloat16 [262144, 128], P(('grp', 'wide')), parts along dimension 0, may hold values from -24 to 24
- block_owner: int32 [32], P('grp'), parts along dimension 0, may hold values from 0 to 15, each once
- block_lengths: int32 [32], P('grp'), parts along dimension 0, may hold values from 1024 to 8192, as said below
- draft_mask: int32 [4, 64, 64], P('grp'), parts along dimension 0, may hold values from 0 to 1, as said below
- out_weight: bfloat16 [4096, 8192], P(None, 'wide'), may hold values from -1 to 1
- norm_gain: float32 [8192], replicated, may hold values from 0.25 to 1.75
- gate_weight: bfloat16 [8192, 14336], P(None, 'wide'), may hold values from -0.0625 to 0.0625
- up_weight: bfloat16 [8192, 14336], P(None, 'wide'), may hold values from -0.0625 to 0.0625
Outputs:
- projected: bfloat16 [256, 8192], P('grp', 'wide'), parts along dimension 0
- hidden: bfloat16 [256, 14336], P('grp', 'wide'), parts along dimension 0
There are 2 independent parts, one for each index of `grp`. A program takes and returns all parts, laid end to end along the dimension named above; an argument that names none is the same for every part. Nothing has to cross between parts.
Inputs may be any that keep to these rules, and one draw needn't show every extreme that they name: `block_owner`: each device holds exactly one block. `block_lengths`: at most 8192 rows a block, and some block has exactly 8192 rows. In each sequence row 0 is the root of a tree in which every other row's parent lies 1 to 4 rows before it; draft_mask[s, i, t] is 1 exactly when t is i or an ancestor of i.
All inputs are finite; a program needn't handle non-finite values.
Results may differ from a plain program's by a relative error of at most 0.02.
Values may be sent and summed in bfloat16 or wider, within the bound.
A program may use at most 128 MiB of HBM per device.

v0:
```python
import math
import jax
import jax.numpy as jnp
from jax import lax
from jax.sharding import PartitionSpec as P

very_low = -1e30
epsilon = 1e-05


def block_update(state, query_rows, block_keys, block_values, valid, scale):
    running, total, weighted = state
    scores = (
        jnp.einsum("igc,kc->igk", query_rows, block_keys, preferred_element_type=jnp.float32)
        * scale
    )
    scores = jnp.where(valid, scores, very_low)
    newest = jnp.maximum(running, jnp.max(scores, axis=-1))
    factor = jnp.exp(running - newest)
    weights = jnp.where(valid, jnp.exp(scores - newest[..., None]), 0.0)
    total = total * factor + jnp.sum(weights, axis=-1)
    weighted = weighted * factor[..., None] + jnp.einsum(
        "igk,kc->igc",
        weights.astype(jnp.bfloat16),
        block_values,
        preferred_element_type=jnp.float32,
    )
    return (newest, total, weighted)


def attend(query_rows, keys, values, length, own_keys, own_values, own_valid):
    block_size = min(512, keys.shape[0])
    scale = 1.0 / math.sqrt(query_rows.shape[2])
    rows_count = query_rows.shape[0]
    heads = query_rows.shape[1]
    state = (
        jnp.full((rows_count, heads), very_low, jnp.float32),
        jnp.zeros((rows_count, heads), jnp.float32),
        jnp.zeros((rows_count, heads, query_rows.shape[2]), jnp.float32),
    )
    offsets = jnp.arange(block_size, dtype=jnp.int32)

    def advance(number, carry):
        begin = (number * block_size).astype(jnp.int32)
        block_keys = lax.dynamic_slice_in_dim(keys, begin, block_size, 0)
        block_values = lax.dynamic_slice_in_dim(values, begin, block_size, 0)
        valid = (begin + offsets < length)[None, None, :]
        return block_update(carry, query_rows, block_keys, block_values, valid, scale)

    count = (length + block_size - 1) // block_size
    state = lax.fori_loop(jnp.int32(0), count, advance, state)
    return block_update(state, query_rows, own_keys, own_values, own_valid[:, None, :], scale)


def per_device(
    queries,
    draft_keys,
    draft_values,
    cache_keys,
    cache_values,
    block_owner,
    block_lengths,
    draft_mask,
    out_weight,
    norm_gain,
    gate_weight,
    up_weight,
):
    devices = lax.axis_size("wide")
    own_index = lax.axis_index("wide")
    head_size = cache_keys.shape[1]
    key_heads = draft_keys.shape[1] // head_size
    group_width = queries.shape[1] // key_heads
    group = group_width // head_size
    sequences = draft_mask.shape[0]
    draft_rows = draft_mask.shape[1]
    all_rows = sequences * draft_rows
    local_rows = queries.shape[0]
    heads_all = key_heads * group
    blocks_per_pair = devices // (sequences * key_heads)
    device_ids = jnp.arange(devices, dtype=jnp.int32)
    owned = (block_owner[None, :] == device_ids[:, None]).astype(jnp.int32)
    device_block = jnp.sum(owned * device_ids[None, :], axis=1)
    device_pair = device_block // blocks_per_pair
    device_sequence = device_pair // key_heads
    device_head = device_pair % key_heads
    device_length = jnp.sum(owned * block_lengths[None, :], axis=1)
    picker = (device_ids == own_index).astype(jnp.int32)
    own_block = jnp.sum(picker * device_block)
    own_sequence = jnp.sum(picker * device_sequence)
    own_head = jnp.sum(picker * device_head)
    own_length = jnp.sum(picker * device_length)
    is_last = own_block % blocks_per_pair == blocks_per_pair - 1
    row_start = own_sequence * draft_rows
    head_numbers = jnp.arange(key_heads, dtype=jnp.int32)
    every_query, every_key, every_value = (
        lax.all_gather(queries, "wide", axis=0, tiled=True),
        lax.all_gather(draft_keys, "wide", axis=0, tiled=True),
        lax.all_gather(draft_values, "wide", axis=0, tiled=True),
    )
    query_columns = own_head * group_width
    key_columns = own_head * head_size
    pair_queries = lax.dynamic_slice_in_dim(
        lax.dynamic_slice_in_dim(every_query, row_start, draft_rows, 0),
        query_columns,
        group_width,
        1,
    )
    pair_keys = lax.dynamic_slice_in_dim(
        lax.dynamic_slice_in_dim(every_key, row_start, draft_rows, 0), key_columns, head_size, 1
    )
    pair_values = lax.dynamic_slice_in_dim(
        lax.dynamic_slice_in_dim(every_value, row_start, draft_rows, 0), key_columns, head_size, 1
    )
    own_head = jnp.sum(picker * device_head)
    query_rows = pair_queries.reshape(draft_rows, group, head_size)
    own_valid = (
        lax.dynamic_index_in_dim(draft_mask, own_sequence, 0, keepdims=False) > 0
    ) & is_last
    running, total, weighted = attend(
        query_rows, cache_keys, cache_values, own_length, pair_keys, pair_values, own_valid
    )
    block_output = (weighted / total[..., None]).astype(jnp.bfloat16)
    slot_peak = lax.dynamic_update_slice(
        jnp.full((all_rows, group), very_low, jnp.float32), running, (row_start, jnp.int32(0))
    ).reshape(devices, local_rows, group)
    slot_total = lax.dynamic_update_slice(
        jnp.zeros((all_rows, group), jnp.float32), total, (row_start, jnp.int32(0))
    ).reshape(devices, local_rows, group)
    slot_output = lax.dynamic_update_slice(
        jnp.zeros((all_rows, group, head_size), jnp.bfloat16),
        block_output,
        (row_start, jnp.int32(0), jnp.int32(0)),
    ).reshape(devices, local_rows, group, head_size)
    back_peak, back_total = (
        lax.all_to_all(slot_peak, "wide", split_axis=0, concat_axis=0, tiled=True),
        lax.all_to_all(slot_total, "wide", split_axis=0, concat_axis=0, tiled=True),
    )
    back_output = lax.all_to_all(slot_output, "wide", split_axis=0, concat_axis=0, tiled=True)
    member = device_head[:, None] == head_numbers[None, :]
    spread = jnp.where(member[:, None, :, None], back_peak[:, :, None, :], very_low)
    highest = jnp.max(spread, axis=0)
    mixing = jnp.exp(spread - highest[None]) * back_total[:, :, None, :]
    row_total = jnp.sum(mixing, axis=0)
    row_weighted = jnp.einsum(
        "srgj,srjc->rgjc", mixing, back_output.astype(jnp.float32), precision=lax.Precision.HIGHEST
    )
    attended_rows = (
        (row_weighted / row_total[..., None])
        .astype(jnp.bfloat16)
        .reshape(local_rows, heads_all * head_size)
    )
    combined = jnp.dot(
        lax.all_gather(attended_rows, "wide", axis=0, tiled=True),
        out_weight,
        preferred_element_type=jnp.float32,
    )
    projected = combined.astype(jnp.bfloat16)
    columns = projected.shape[1]
    branch = lax.optimization_barrier(projected).astype(jnp.float32)
    squares = lax.psum(jnp.sum(branch * branch, axis=1), "wide")
    inverse = lax.rsqrt(squares / (columns * devices) + epsilon)
    gain_part = lax.dynamic_slice_in_dim(norm_gain, own_index * columns, columns, 0)
    normed = (branch * inverse[:, None] * gain_part[None, :]).astype(jnp.bfloat16)
    piece = lax.all_gather(normed, "wide", axis=1, tiled=True)
    gate = jnp.dot(piece, gate_weight, preferred_element_type=jnp.float32)
    upward = jnp.dot(piece, up_weight, preferred_element_type=jnp.float32)
    hidden = (jax.nn.silu(gate) * upward).astype(jnp.bfloat16)
    return (projected, hidden)


def solution(mesh):
    placed = (
        P(("grp", "wide"), None),
        P(("grp", "wide"), None),
        P(("grp", "wide"), None),
        P(("grp", "wide"), None),
        P(("grp", "wide"), None),
        P("grp"),
        P("grp"),
        P("grp", None, None),
        P(None, "wide"),
        P(),
        P(None, "wide"),
        P(None, "wide"),
    )
    return jax.shard_map(
        per_device,
        mesh=mesh,
        in_specs=placed,
        out_specs=(P("grp", "wide"), P("grp", "wide")),
        check_vma=False,
    )
```

profile of v0, /device:TPU:0, one launch (start us, length us, event | category | flops | bytes accessed | tf_op | source)
XLA Modules:
  0.0 300.9 jit_solution(8862913507777741700)
XLA Ops:
  7.9 0.8 select_reduce_fusion.2
  8.7 0.8 select_reduce_fusion.4
  16.7 23.9 %all_gather.16 = bf16[128,512]{1,0:T(8,128)(2,1)S(1)} all-gather(bf16[8,512]{1,0:T(8,128)(2,1)} %param.15), channel_id=1, replica_groups=mesh['grp'=2,'wide'=16] {'wide'}, dimensions={0}, use_global_device_ids=true | all-gather | bytes 139264 | tf_op jit(solution)/shard_map/all_gather | solution.py:98
  40.6 0.8 fusion.41
  41.4 9.5 %all-gather.4.cloned.1.call-done = bf16[128,4096]{1,0:T(8,128)(2,1)} async-done(((bf16[8,4096]{1,0:T(8,128)(2,1)}), bf16[128,4096]{1,0:T(8,128)(2,1)}) %all-gather.4.cloned.1.call-update) | async-done | bytes 1048592 | tf_op jit(solution)/shard_map/all_gather | solution.py:97
  50.9 1.0 dynamic-slice_bitcast_fusion.1
  52.5 11.5 %while.15 = (s32[]{:T(128)}, f32[64,8]{0,1:T(8,128)S(1)}, f32[64,8]{0,1:T(8,128)S(1)}, f32[64,8,128]{2,1,0:T(8,128)S(1)}, s32[]{:T(128)}, /*index=5*/s32[]{:T(12...) while((s32[]{:T(128)}, f32[64,8]{0,1:T(8,128)S(1)}, ...), condition=%wide.region_8.9_spmd.clone, body=%wide.region_5.8_spmd.clone.sunk | while | flops 136185856 | bytes 4099771 | solution.py:51
  52.5 0.7 fusion.68
  53.3 1.3 fusion.69
  55.0 1.3 convolution_add_fusion.3
  56.4 0.7 fusion.68
  57.1 1.3 fusion.69
  58.9 1.3 convolution_add_fusion.3
  60.2 0.7 fusion.68
  60.9 1.3 fusion.69
  62.7 1.3 convolution_add_fusion.3
  65.5 52.4 %all-to-all-start.2 = ((f32[16,8,8]{1,2,0:T(8,128)}), f32[16,8,8]{1,2,0:T(8,128)S(1)}, u32[]{:S(2)}, u32[]{:S(2)}) async-start(f32[16,8,8]{1,2,0:T(8,128)} %copy.68), calls=%async_computation.2 | async-start | bytes 131072 | tf_op jit(solution)/shard_map/all_to_all | solution.py:137
  117.9 22.1 %all_gather.17 = bf16[128,512]{1,0:T(8,128)(2,1)S(1)} all-gather(bf16[8,512]{1,0:T(8,128)(2,1)S(1)} %copy-done.2), channel_id=1, replica_groups=mesh['grp'=2,'wide'=16] {'wide'}, dimensions={0}, use_global_device_ids=true | all-gather | bytes 139264 | tf_op jit(solution)/shard_map/all_gather | solution.py:99
  141.1 3.5 %all-to-all-start.1 = ((f32[16,8,8]{1,2,0:T(8,128)}), f32[16,8,8]{1,2,0:T(8,128)S(1)}, u32[]{:S(2)}, u32[]{:S(2)}) async-start(f32[16,8,8]{1,2,0:T(8,128)} %copy.66), calls=%async_computation.1 | async-start | bytes 131072 | tf_op jit(solution)/shard_map/all_to_all | solution.py:136
  144.6 0.7 broadcast_in_dim.96
  145.4 0.9 fusion.18
  146.3 5.2 %all-to-all-done.1 = f32[16,8,8]{1,2,0:T(8,128)S(1)} async-done(((f32[16,8,8]{1,2,0:T(8,128)}), f32[16,8,8]{1,2,0:T(8,128)S(1)}, u32[]{:S(2)}, u32[]{:S(2)}) %all-to-all-start.1) | async-done | bytes 4128 | tf_op jit(solution)/shard_map/all_to_all | solution.py:136
  151.5 3.5 %all-to-all-start = ((bf16[16,8,8,128]{3,2,1,0:T(8,128)(2,1)}), bf16[16,8,8,128]{3,2,1,0:T(8,128)(2,1)S(1)}, u32[]{:S(2)}, u32[]{:S(2)}) async-start(bf16[16,8,8,128]{3,2,1,0:T(8,128)(2,1)} %bitcast.3), calls=%async_computation | async-start | bytes 524288 | tf_op jit(solution)/shard_map/all_to_all | solution.py:139
  155.7 9.3 %all-to-all-done = bf16[16,8,8,128]{3,2,1,0:T(8,128)(2,1)S(1)} async-done(((bf16[16,8,8,128]{3,2,1,0:T(8,128)(2,1)}), bf16[16,8,8,128]{3,2,1,0:T(8,128)(2,1)S(1)}, u32[]{:S(2)}, u32[]{:S(2)}) %all-to-all-start) | async-done | bytes 262176 | tf_op jit(solution)/shard_map/all_to_all | solution.py:139
  166.3 0.8 dynamic_slice.29
  167.1 36.5 %all-gather.6.cloned.1.call-done = bf16[128,4096]{1,0:T(8,128)(2,1)} async-done(((bf16[8,4096]{1,0:T(8,128)(2,1)}), bf16[128,4096]{1,0:T(8,128)(2,1)}) %all-gather.6.cloned.1.call-update) | async-done | bytes 1048592 | tf_op jit(solution)/shard_map/all_gather | solution.py:154
  203.5 3.2 %convolution_convert_fusion = bf16[128,512]{1,0:T(8,128)(2,1)S(1)} fusion(bf16[128,4096]{1,0:T(8,128)(2,1)} %all-gather.6.cloned.1.call-done, bf16[4096,512]{1,0:T(8,128)(2,1)} %param.22), kind=kOutput, calls=%fused_computation.27 | convolution fusion | flops 536936448 | bytes 5373952 | tf_op jit(solution)/shard_map/dot_general | solution.py:153
  206.9 31.6 %psum.7 = f32[128]{0:T(128)S(1)} all-reduce(f32[128]{0:T(128)S(1)} %fusion.21), channel_id=1, replica_groups=mesh['grp'=2,'wide'=16] {'wide'}, use_global_device_ids=true, to_apply=%region_15.16 | all-reduce | flops 128 | bytes 1024 | tf_op jit(solution)/shard_map/psum | solution.py:161
  238.5 0.8 fusion.23
  239.3 38.4 %all-gather.8.cloned.1.call-done = bf16[128,8192]{1,0:T(8,128)(2,1)} async-done(((bf16[128,512]{1,0:T(8,128)(2,1)}), bf16[128,8192]{1,0:T(8,128)(2,1)}) %all-gather.8.cloned.1.call-update) | async-done | bytes 2097168 | tf_op jit(solution)/shard_map/all_gather | solution.py:165
  277.7 8.3 %fusion.50 = f32[128,896]{1,0:T(8,128)S(1)} fusion(bf16[128,8192]{1,0:T(8,128)(2,1)} %all-gather.8.cloned.1.call-done, bf16[8192,896]{1,0:T(8,128)(2,1)} %param.24), kind=kOutput, calls=%fused_computation.90 | convolution fusion | flops 1879048192 | bytes 17235968 | tf_op jit(solution)/shard_map/dot_general | solution.py:166
  286.1 8.3 %fusion.14 = bf16[128,896]{1,0:T(8,128)(2,1)} fusion(bf16[128,8192]{1,0:T(8,128)(2,1)S(1)} %copy-done, bf16[8192,896]{1,0:T(8,128)(2,1)} %param.25, f32[128,896]{1,0:T(8,128)S(1)} %fusion.50), kind=kOutput, calls=%fused_computation.20 | convolution fusion | flops 1879736320 | bytes 17465344 | tf_op jit(solution)/shard_map/dot_general | solution.py:167
  (61 shorter events, 7.9 us)
Async XLA Ops:
  7.2 43.8 %all-gather.4.cloned.1.call-start = ((), (), s32[]{:S(2)}) async-start(), calls=%async_computation.3 | async-start | bytes 1114112 | tf_op jit(solution)/shard_map/all_gather | solution.py:97
  52.5 65.3 %copy-start.2 = (bf16[8,512]{1,0:T(8,128)(2,1)S(1)}, bf16[8,512]{1,0:T(8,128)(2,1)}, u32[]{:S(2)}) copy-start(bf16[8,512]{1,0:T(8,128)(2,1)} %param.16) | copy-start | bytes 24580
  65.5 75.7 %all-to-all-start.2 = ((f32[16,8,8]{1,2,0:T(8,128)}), f32[16,8,8]{1,2,0:T(8,128)S(1)}, u32[]{:S(2)}, u32[]{:S(2)}) async-start(f32[16,8,8]{1,2,0:T(8,128)} %copy.68), calls=%async_computation.2 | async-start | bytes 131072 | tf_op jit(solution)/shard_map/all_to_all | solution.py:137
  141.1 10.4 %all-to-all-start.1 = ((f32[16,8,8]{1,2,0:T(8,128)}), f32[16,8,8]{1,2,0:T(8,128)S(1)}, u32[]{:S(2)}, u32[]{:S(2)}) async-start(f32[16,8,8]{1,2,0:T(8,128)} %copy.66), calls=%async_computation.1 | async-start | bytes 131072 | tf_op jit(solution)/shard_map/all_to_all | solution.py:136
  151.5 13.5 %all-to-all-start = ((bf16[16,8,8,128]{3,2,1,0:T(8,128)(2,1)}), bf16[16,8,8,128]{3,2,1,0:T(8,128)(2,1)S(1)}, u32[]{:S(2)}, u32[]{:S(2)}) async-start(bf16[16,8,8,128]{3,2,1,0:T(8,128)(2,1)} %bitcast.3), calls=%async_computation | async-start | bytes 524288 | tf_op jit(solution)/shard_map/all_to_all | solution.py:139
  155.0 48.5 %all-gather.6.cloned.1.call-start = ((), (), s32[]{:S(2)}) async-start(), calls=%async_computation.4 | async-start | bytes 1114112 | tf_op jit(solution)/shard_map/all_gather | solution.py:154
  166.3 111.5 %all-gather.8.cloned.1.call-start = ((), (), s32[]{:S(2)}) async-start(), calls=%async_computation.5 | async-start | bytes 2228224 | tf_op jit(solution)/shard_map/all_gather | solution.py:165
  206.8 79.3 %copy-start.1 = (bf16[128,512]{1,0:T(8,128)(2,1)}, bf16[128,512]{1,0:T(8,128)(2,1)S(1)}, u32[]{:S(2)}) copy-start(bf16[128,512]{1,0:T(8,128)(2,1)S(1)} %convolution_convert_fusion) | copy-start | bytes 393220
  277.7 8.3 %copy-start = (bf16[128,8192]{1,0:T(8,128)(2,1)S(1)}, bf16[128,8192]{1,0:T(8,128)(2,1)}, u32[]{:S(2)}) copy-start(bf16[128,8192]{1,0:T(8,128)(2,1)} %all-gather.8.cloned.1.call-done) | copy-start | bytes 6291460
Sparse Core Ops, SparseCore 0:
  10.1 40.7 all-gather.3
  166.4 37.1 all-gather.5
  239.4 38.2 all-gather.7
where the time goes:
time: 302 us; the launch traced here: 301 us
  waiting for transfers between devices  99.6 us (33%)
  blocking collectives  77.6 us (26%)
  starting transfers between devices  59.5 us (20%)
  matrix products  29.6 us (10%)
  between operations  20.6 us (7%)
  other arithmetic  7.69 us (3%)
  local copies, waits for them, and re-layouts  6.13 us (2%)
    all_to_all x1, starting transfers between devices, per_device(): lax.all_to_all(slot_total, 'wide', split_axis=0, concat_axis=0, tiled=True)  52.4 us
    all_gather x1, waiting for transfers between devices, per_device(): piece = lax.all_gather(normed, 'wide', axis=1, tiled=True)  38.4 us
    all_gather x1, waiting for transfers between devices, per_device(): lax.all_gather(attended_rows, 'wide', axis=0, tiled=True)  36.5 us
    psum x1, blocking collectives, per_device(): squares = lax.psum(jnp.sum(branch * branch, axis=1), 'wide')  31.6 us
    all_gather x1, blocking collectives, per_device(): lax.all_gather(draft_keys, 'wide', axis=0, tiled=True)  23.9 us
    all_gather x1, blocking collectives, per_device(): lax.all_gather(draft_values, 'wide', axis=0, tiled=True)  22.1 us
    all_gather x1, waiting for transfers between devices, per_device(): lax.all_gather(queries, 'wide', axis=0, tiled=True)  9.54 us
    all_to_all x1, waiting for transfers between devices, per_device(): lax.all_to_all(slot_output, 'wide', split_axis=0, concat_axis=0, tiled=True)  9.29 us
  transfers between devices with their start and end apart: 6, of which 5 were waited for; matrix products, arithmetic and copies ran while one was open for 2% of the time, Pallas kernels for 0%

commit v1 on v0

--- a/solution.py
+++ b/solution.py
@@ -162,7 +162,12 @@
     inverse = lax.rsqrt(squares / (columns * devices) + epsilon)
     gain_part = lax.dynamic_slice_in_dim(norm_gain, own_index * columns, columns, 0)
     normed = (branch * inverse[:, None] * gain_part[None, :]).astype(jnp.bfloat16)
-    piece = lax.all_gather(normed, "wide", axis=1, tiled=True)
+    ring = [normed]
+    for hop in range(15):
+        ring.append(lax.ppermute(ring[-1], "wide", [(dev, (dev + 1) % 16) for dev in range(16)]))
+    piece = jnp.roll(
+        jnp.concatenate(ring[::-1], axis=1), (lax.axis_index("wide") + 1) * ring[0].shape[1], axis=1
+    )
     gate = jnp.dot(piece, gate_weight, preferred_element_type=jnp.float32)
     upward = jnp.dot(piece, up_weight, preferred_element_type=jnp.float32)
     hidden = (jax.nn.silu(gate) * upward).astype(jnp.bfloat16)

time: 302 us -> 366 us (1.21)
  waiting for transfers between devices: 99.6 us -> 168 us
  matrix products: 29.6 us -> 23.8 us
    ppermute x0 -> x15, waiting for transfers between devices: none -> 106 us  [per_device(): lax.ppermute(ring[-1], 'wide', [(dev, (dev + 1) % 16) for dev in range(16)])]
    all_gather x1 -> x0, waiting for transfers between devices: 38.4 us -> none  [per_device(): piece = lax.all_gather(normed, 'wide', axis=1, tiled=True)]
    dot_general x1, matrix products: 8.32 us -> 3.16 us  [per_device(): upward = jnp.dot(piece, up_weight, preferred_element_type=jnp.float32)]
  transfers between devices with their start and end apart: 6 -> 20, of which waited for: 5 -> 19; matrix products, arithmetic and copies ran while one was open for 2% -> 2% of each run, Pallas kernels for 0% -> 0%
where the time goes in v1:
time: 366 us; the launch traced here: 365 us
  waiting for transfers between devices  168 us (46%)
  blocking collectives  77.5 us (21%)
  starting transfers between devices  59.5 us (16%)
  matrix products  23.8 us (7%)
  between operations  21.2 us (6%)
  local copies, waits for them, and re-layouts  7.97 us (2%)
  other arithmetic  7.19 us (2%)
    ppermute x15, waiting for transfers between devices, per_device(): lax.ppermute(ring[-1], 'wide', [(dev, (dev + 1) % 16) for dev in range(16)])  106 us
    all_to_all x1, starting transfers between devices, per_device(): lax.all_to_all(slot_total, 'wide', split_axis=0, concat_axis=0, tiled=True)  52.3 us
    all_gather x1, waiting for transfers between devices, per_device(): lax.all_gather(attended_rows, 'wide', axis=0, tiled=True)  36.5 us
    psum x1, blocking collectives, per_device(): squares = lax.psum(jnp.sum(branch * branch, axis=1), 'wide')  31.6 us
    all_gather x1, blocking collectives, per_device(): lax.all_gather(draft_keys, 'wide', axis=0, tiled=True)  23.9 us
    all_gather x1, blocking collectives, per_device(): lax.all_gather(draft_values, 'wide', axis=0, tiled=True)  22.1 us
    all_gather x1, waiting for transfers between devices, per_device(): lax.all_gather(queries, 'wide', axis=0, tiled=True)  9.61 us
    all_to_all x1, waiting for transfers between devices, per_device(): lax.all_to_all(slot_output, 'wide', split_axis=0, concat_axis=0, tiled=True)  9.29 us
  transfers between devices with their start and end apart: 20, of which 19 were waited for; matrix products, arithmetic and copies ran while one was open for 2% of the time, Pallas kernels for 0%

profile of v1, /device:TPU:0, one launch (start us, length us, event | category | flops | bytes accessed | tf_op | source)
XLA Modules:
  0.0 365.0 jit_solution(14037851647861395135)
XLA Ops:
  16.7 23.9 %all_gather.13 = bf16[128,512]{1,0:T(8,128)(2,1)S(1)} all-gather(bf16[8,512]{1,0:T(8,128)(2,1)} %param.15), channel_id=1, replica_groups=mesh['grp'=2,'wide'=16] {'wide'}, dimensions={0}, use_global_device_ids=true | all-gather | bytes 139264 | tf_op jit(solution)/shard_map/all_gather | solution.py:98
  41.3 9.6 %all-gather.3.cloned.1.call-done = bf16[128,4096]{1,0:T(8,128)(2,1)} async-done(((bf16[8,4096]{1,0:T(8,128)(2,1)}), bf16[128,4096]{1,0:T(8,128)(2,1)}) %all-gather.3.cloned.1.call-update) | async-done | bytes 1048592 | tf_op jit(solution)/shard_map/all_gather | solution.py:97
  52.5 11.5 %while.15 = (s32[]{:T(128)}, f32[64,8]{0,1:T(8,128)S(1)}, f32[64,8]{0,1:T(8,128)S(1)}, f32[64,8,128]{2,1,0:T(8,128)S(1)}, s32[]{:T(128)}, /*index=5*/s32[]{:T(12...) while((s32[]{:T(128)}, f32[64,8]{0,1:T(8,128)S(1)}, ...), condition=%wide.region_8.9_spmd.clone, body=%wide.region_5.8_spmd.clone.sunk | while | flops 136185856 | bytes 4099771 | solution.py:51
  55.0 1.3 convolution_add_fusion.3
  58.8 1.3 convolution_add_fusion.3
  62.7 1.3 convolution_add_fusion.3
  65.5 52.3 %all-to-all-start.2 = ((f32[16,8,8]{1,2,0:T(8,128)}), f32[16,8,8]{1,2,0:T(8,128)S(1)}, u32[]{:S(2)}, u32[]{:S(2)}) async-start(f32[16,8,8]{1,2,0:T(8,128)} %copy.68), calls=%async_computation.2 | async-start | bytes 131072 | tf_op jit(solution)/shard_map/all_to_all | solution.py:137
  117.8 22.1 %all_gather.14 = bf16[128,512]{1,0:T(8,128)(2,1)S(1)} all-gather(bf16[8,512]{1,0:T(8,128)(2,1)S(1)} %copy-done.1), channel_id=1, replica_groups=mesh['grp'=2,'wide'=16] {'wide'}, dimensions={0}, use_global_device_ids=true | all-gather | bytes 139264 | tf_op jit(solution)/shard_map/all_gather | solution.py:99
  141.0 3.5 all-to-all-start.1
  146.2 5.2 %all-to-all-done.1 = f32[16,8,8]{1,2,0:T(8,128)S(1)} async-done(((f32[16,8,8]{1,2,0:T(8,128)}), f32[16,8,8]{1,2,0:T(8,128)S(1)}, u32[]{:S(2)}, u32[]{:S(2)}) %all-to-all-start.1) | async-done | bytes 4128 | tf_op jit(solution)/shard_map/all_to_all | solution.py:136
  151.4 3.5 all-to-all-start
  155.6 9.3 %all-to-all-done = bf16[16,8,8,128]{3,2,1,0:T(8,128)(2,1)S(1)} async-done(((bf16[16,8,8,128]{3,2,1,0:T(8,128)(2,1)}), bf16[16,8,8,128]{3,2,1,0:T(8,128)(2,1)S(1)}, u32[]{:S(2)}, u32[]{:S(2)}) %all-to-all-start) | async-done | bytes 262176 | tf_op jit(solution)/shard_map/all_to_all | solution.py:139
  167.0 36.5 %all-gather.5.cloned.1.call-done = bf16[128,4096]{1,0:T(8,128)(2,1)} async-done(((bf16[8,4096]{1,0:T(8,128)(2,1)}), bf16[128,4096]{1,0:T(8,128)(2,1)}) %all-gather.5.cloned.1.call-update) | async-done | bytes 1048592 | tf_op jit(solution)/shard_map/all_gather | solution.py:154
  203.5 3.2 convolution_convert_fusion
  206.9 31.6 %psum.7 = f32[128]{0:T(128)S(1)} all-reduce(f32[128]{0:T(128)S(1)} %fusion.24), channel_id=1, replica_groups=mesh['grp'=2,'wide'=16] {'wide'}, use_global_device_ids=true, to_apply=%region_15.16 | all-reduce | flops 128 | bytes 1024 | tf_op jit(solution)/shard_map/psum | solution.py:161
  238.6 7.1 %collective-permute-done = bf16[128,512]{1,0:T(8,128)(2,1)S(1)} collective-permute-done((bf16[128,512]{1,0:T(8,128)(2,1)S(1)}, bf16[128,512]{1,0:T(8,128)(2,1)S(1)}, u32[]{:S(2)}, u32[]{:S(2)}) %collective-permute-start) | collective-permute-done | bytes 131104 | tf_op jit(solution)/shard_map/ppermute | solution.py:167
  245.7 7.1 %collective-permute-done.1 = bf16[128,512]{1,0:T(8,128)(2,1)S(1)} collective-permute-done((bf16[128,512]{1,0:T(8,128)(2,1)S(1)}, bf16[128,512]{1,0:T(8,128)(2,1)S(1)}, u32[]{:S(2)}, u32[]{:S(2)}) %collective-permute-start.1) | collective-permute-done | bytes 131104 | tf_op jit(solution)/shard_map/ppermute | solution.py:167
  252.8 7.1 %collective-permute-done.2 = bf16[128,512]{1,0:T(8,128)(2,1)S(1)} collective-permute-done((bf16[128,512]{1,0:T(8,128)(2,1)S(1)}, bf16[128,512]{1,0:T(8,128)(2,1)S(1)}, u32[]{:S(2)}, u32[]{:S(2)}) %collective-permute-start.2) | collective-permute-done | bytes 131104 | tf_op jit(solution)/shard_map/ppermute | solution.py:167
  259.9 7.1 %collective-permute-done.3 = bf16[128,512]{1,0:T(8,128)(2,1)S(1)} collective-permute-done((bf16[128,512]{1,0:T(8,128)(2,1)S(1)}, bf16[128,512]{1,0:T(8,128)(2,1)S(1)}, u32[]{:S(2)}, u32[]{:S(2)}) %collective-permute-start.3) | collective-permute-done | bytes 131104 | tf_op jit(solution)/shard_map/ppermute | solution.py:167
  267.0 7.1 %collective-permute-done.4 = bf16[128,512]{1,0:T(8,128)(2,1)S(1)} collective-permute-done((bf16[128,512]{1,0:T(8,128)(2,1)S(1)}, bf16[128,512]{1,0:T(8,128)(2,1)S(1)}, u32[]{:S(2)}, u32[]{:S(2)}) %collective-permute-start.4) | collective-permute-done | bytes 131104 | tf_op jit(solution)/shard_map/ppermute | solution.py:167
  274.1 7.1 %collective-permute-done.5 = bf16[128,512]{1,0:T(8,128)(2,1)S(1)} collective-permute-done((bf16[128,512]{1,0:T(8,128)(2,1)S(1)}, bf16[128,512]{1,0:T(8,128)(2,1)S(1)}, u32[]{:S(2)}, u32[]{:S(2)}) %collective-permute-start.5) | collective-permute-done | bytes 131104 | tf_op jit(solution)/shard_map/ppermute | solution.py:167
  281.2 7.1 %collective-permute-done.6 = bf16[128,512]{1,0:T(8,128)(2,1)S(1)} collective-permute-done((bf16[128,512]{1,0:T(8,128)(2,1)S(1)}, bf16[128,512]{1,0:T(8,128)(2,1)S(1)}, u32[]{:S(2)}, u32[]{:S(2)}) %collective-permute-start.6) | collective-permute-done | bytes 131104 | tf_op jit(solution)/shard_map/ppermute | solution.py:167
  288.3 7.1 %collective-permute-done.7 = bf16[128,512]{1,0:T(8,128)(2,1)S(1)} collective-permute-done((bf16[128,512]{1,0:T(8,128)(2,1)S(1)}, bf16[128,512]{1,0:T(8,128)(2,1)S(1)}, u32[]{:S(2)}, u32[]{:S(2)}) %collective-permute-start.7) | collective-permute-done | bytes 131104 | tf_op jit(solution)/shard_map/ppermute | solution.py:167
  295.4 7.1 %collective-permute-done.8 = bf16[128,512]{1,0:T(8,128)(2,1)S(1)} collective-permute-done((bf16[128,512]{1,0:T(8,128)(2,1)S(1)}, bf16[128,512]{1,0:T(8,128)(2,1)S(1)}, u32[]{:S(2)}, u32[]{:S(2)}) %collective-permute-start.8) | collective-permute-done | bytes 131104 | tf_op jit(solution)/shard_map/ppermute | solution.py:167
  302.4 7.1 %collective-permute-done.9 = bf16[128,512]{1,0:T(8,128)(2,1)S(1)} collective-permute-done((bf16[128,512]{1,0:T(8,128)(2,1)S(1)}, bf16[128,512]{1,0:T(8,128)(2,1)S(1)}, u32[]{:S(2)}, u32[]{:S(2)}) %collective-permute-start.9) | collective-permute-done | bytes 131104 | tf_op jit(solution)/shard_map/ppermute | solution.py:167
  309.5 7.1 %collective-permute-done.10 = bf16[128,512]{1,0:T(8,128)(2,1)S(1)} collective-permute-done((bf16[128,512]{1,0:T(8,128)(2,1)S(1)}, bf16[128,512]{1,0:T(8,128)(2,1)S(1)}, u32[]{:S(2)}, u32[]{:S(2)}) %collective-permute-start.10) | collective-permute-done | bytes 131104 | tf_op jit(solution)/shard_map/ppermute | solution.py:167
  316.6 7.1 %collective-permute-done.11 = bf16[128,512]{1,0:T(8,128)(2,1)S(1)} collective-permute-done((bf16[128,512]{1,0:T(8,128)(2,1)S(1)}, bf16[128,512]{1,0:T(8,128)(2,1)S(1)}, u32[]{:S(2)}, u32[]{:S(2)}) %collective-permute-start.11) | collective-permute-done | bytes 131104 | tf_op jit(solution)/shard_map/ppermute | solution.py:167
  323.7 7.1 %collective-permute-done.12 = bf16[128,512]{1,0:T(8,128)(2,1)S(1)} collective-permute-done((bf16[128,512]{1,0:T(8,128)(2,1)S(1)}, bf16[128,512]{1,0:T(8,128)(2,1)S(1)}, u32[]{:S(2)}, u32[]{:S(2)}) %collective-permute-start.12) | collective-permute-done | bytes 131104 | tf_op jit(solution)/shard_map/ppermute | solution.py:167
  330.8 7.1 %collective-permute-done.13 = bf16[128,512]{1,0:T(8,128)(2,1)S(1)} collective-permute-done((bf16[128,512]{1,0:T(8,128)(2,1)S(1)}, bf16[128,512]{1,0:T(8,128)(2,1)S(1)}, u32[]{:S(2)}, u32[]{:S(2)}) %collective-permute-start.13) | collective-permute-done | bytes 131104 | tf_op jit(solution)/shard_map/ppermute | solution.py:167
  337.9 7.1 %collective-permute-done.14 = bf16[128,512]{1,0:T(8,128)(2,1)S(1)} collective-permute-done((bf16[128,512]{1,0:T(8,128)(2,1)S(1)}, bf16[128,512]{1,0:T(8,128)(2,1)S(1)}, u32[]{:S(2)}, u32[]{:S(2)}) %collective-permute-start.14) | collective-permute-done | bytes 131104 | tf_op jit(solution)/shard_map/ppermute | solution.py:167
  345.8 7.7 %fusion.16 = f32[128,896]{1,0:T(8,128)S(1)} fusion(bf16[8192,896]{1,0:T(8,128)(2,1)} %param.24, bf16[128,16384]{1,0:T(8,128)(2,1)S(1)} %constant_dynamic-update-slice_fusion, s32[]{:T(128)S(6)} %select_n.115), kind=kOutput, calls=%fused_computation.21 | convolution fusion | flops 1879048192 | bytes 17235972 | tf_op jit(solution)/shard_map/dot_general | solution.py:171
  355.0 3.2 multiply_convert_fusion
  (127 shorter events, 21.8 us)
Async XLA Ops:
  7.2 43.8 %all-gather.3.cloned.1.call-start = ((), (), s32[]{:S(2)}) async-start(), calls=%async_computation.3 | async-start | bytes 1114112 | tf_op jit(solution)/shard_map/all_gather | solution.py:97
  52.5 65.3 %copy-start.1 = (bf16[8,512]{1,0:T(8,128)(2,1)S(1)}, bf16[8,512]{1,0:T(8,128)(2,1)}, u32[]{:S(2)}) copy-start(bf16[8,512]{1,0:T(8,128)(2,1)} %param.16) | copy-start | bytes 24580
  65.5 75.6 %all-to-all-start.2 = ((f32[16,8,8]{1,2,0:T(8,128)}), f32[16,8,8]{1,2,0:T(8,128)S(1)}, u32[]{:S(2)}, u32[]{:S(2)}) async-start(f32[16,8,8]{1,2,0:T(8,128)} %copy.68), calls=%async_computation.2 | async-start | bytes 131072 | tf_op jit(solution)/shard_map/all_to_all | solution.py:137
  141.0 10.4 %all-to-all-start.1 = ((f32[16,8,8]{1,2,0:T(8,128)}), f32[16,8,8]{1,2,0:T(8,128)S(1)}, u32[]{:S(2)}, u32[]{:S(2)}) async-start(f32[16,8,8]{1,2,0:T(8,128)} %copy.66), calls=%async_computation.1 | async-start | bytes 131072 | tf_op jit(solution)/shard_map/all_to_all | solution.py:136
  151.4 13.5 %all-to-all-start = ((bf16[16,8,8,128]{3,2,1,0:T(8,128)(2,1)}), bf16[16,8,8,128]{3,2,1,0:T(8,128)(2,1)S(1)}, u32[]{:S(2)}, u32[]{:S(2)}) async-start(bf16[16,8,8,128]{3,2,1,0:T(8,128)(2,1)} %bitcast.3), calls=%async_computation | async-start | bytes 524288 | tf_op jit(solution)/shard_map/all_to_all | solution.py:139
  155.0 48.5 %all-gather.5.cloned.1.call-start = ((), (), s32[]{:S(2)}) async-start(), calls=%async_computation.4 | async-start | bytes 1114112 | tf_op jit(solution)/shard_map/all_gather | solution.py:154
  206.7 138.9 %copy-start = (bf16[128,512]{1,0:T(8,128)(2,1)}, bf16[128,512]{1,0:T(8,128)(2,1)S(1)}, u32[]{:S(2)}) copy-start(bf16[128,512]{1,0:T(8,128)(2,1)S(1)} %convolution_convert_fusion) | copy-start | bytes 393220
  238.6 7.1 %collective-permute-start = (bf16[128,512]{1,0:T(8,128)(2,1)S(1)}, bf16[128,512]{1,0:T(8,128)(2,1)S(1)}, u32[]{:S(2)}, u32[]{:S(2)}) collective-permute-start(bf16[128,512]{1,0:T(8,128)(2,1)S(1)} %fusion.26), channel_id=1, source_target_pairs={{0,1},{1,2},{2,3},{3,4},{4,5},{5,6},{6,7},{7,8},{8,9},{9,10},{10,1... | collective-permute-start | bytes 393224 | tf_op jit(solution)/shard_map/ppermute | solution.py:167
  245.7 7.1 %collective-permute-start.1 = (bf16[128,512]{1,0:T(8,128)(2,1)S(1)}, bf16[128,512]{1,0:T(8,128)(2,1)S(1)}, u32[]{:S(2)}, u32[]{:S(2)}) collective-permute-start(bf16[128,512]{1,0:T(8,128)(2,1)S(1)} %collective-permute-done), channel_id=1, source_target_pairs={{0,1},{1,2},{2,3},{3,4},{4,5},{5,6},{6,7},{7,8},{8,9},{9,10},{10,1... | collective-permute-start | bytes 393224 | tf_op jit(solution)/shard_map/ppermute | solution.py:167
  252.8 7.1 %collective-permute-start.2 = (bf16[128,512]{1,0:T(8,128)(2,1)S(1)}, bf16[128,512]{1,0:T(8,128)(2,1)S(1)}, u32[]{:S(2)}, u32[]{:S(2)}) collective-permute-start(bf16[128,512]{1,0:T(8,128)(2,1)S(1)} %collective-permute-done.1), channel_id=1, source_target_pairs={{0,1},{1,2},{2,3},{3,4},{4,5},{5,6},{6,7},{7,8},{8,9},{9,10},{10,1... | collective-permute-start | bytes 393224 | tf_op jit(solution)/shard_map/ppermute | solution.py:167
  259.9 7.1 %collective-permute-start.3 = (bf16[128,512]{1,0:T(8,128)(2,1)S(1)}, bf16[128,512]{1,0:T(8,128)(2,1)S(1)}, u32[]{:S(2)}, u32[]{:S(2)}) collective-permute-start(bf16[128,512]{1,0:T(8,128)(2,1)S(1)} %collective-permute-done.2), channel_id=1, source_target_pairs={{0,1},{1,2},{2,3},{3,4},{4,5},{5,6},{6,7},{7,8},{8,9},{9,10},{10,1... | collective-permute-start | bytes 393224 | tf_op jit(solution)/shard_map/ppermute | solution.py:167
  267.0 7.1 %collective-permute-start.4 = (bf16[128,512]{1,0:T(8,128)(2,1)S(1)}, bf16[128,512]{1,0:T(8,128)(2,1)S(1)}, u32[]{:S(2)}, u32[]{:S(2)}) collective-permute-start(bf16[128,512]{1,0:T(8,128)(2,1)S(1)} %collective-permute-done.3), channel_id=1, source_target_pairs={{0,1},{1,2},{2,3},{3,4},{4,5},{5,6},{6,7},{7,8},{8,9},{9,10},{10,1... | collective-permute-start | bytes 393224 | tf_op jit(solution)/shard_map/ppermute | solution.py:167
  274.1 7.1 %collective-permute-start.5 = (bf16[128,512]{1,0:T(8,128)(2,1)S(1)}, bf16[128,512]{1,0:T(8,128)(2,1)S(1)}, u32[]{:S(2)}, u32[]{:S(2)}) collective-permute-start(bf16[128,512]{1,0:T(8,128)(2,1)S(1)} %collective-permute-done.4), channel_id=1, source_target_pairs={{0,1},{1,2},{2,3},{3,4},{4,5},{5,6},{6,7},{7,8},{8,9},{9,10},{10,1... | collective-permute-start | bytes 393224 | tf_op jit(solution)/shard_map/ppermute | solution.py:167
  281.2 7.1 %collective-permute-start.6 = (bf16[128,512]{1,0:T(8,128)(2,1)S(1)}, bf16[128,512]{1,0:T(8,128)(2,1)S(1)}, u32[]{:S(2)}, u32[]{:S(2)}) collective-permute-start(bf16[128,512]{1,0:T(8,128)(2,1)S(1)} %collective-permute-done.5), channel_id=1, source_target_pairs={{0,1},{1,2},{2,3},{3,4},{4,5},{5,6},{6,7},{7,8},{8,9},{9,10},{10,1... | collective-permute-start | bytes 393224 | tf_op jit(solution)/shard_map/ppermute | solution.py:167
  288.3 7.1 %collective-permute-start.7 = (bf16[128,512]{1,0:T(8,128)(2,1)S(1)}, bf16[128,512]{1,0:T(8,128)(2,1)S(1)}, u32[]{:S(2)}, u32[]{:S(2)}) collective-permute-start(bf16[128,512]{1,0:T(8,128)(2,1)S(1)} %collective-permute-done.6), channel_id=1, source_target_pairs={{0,1},{1,2},{2,3},{3,4},{4,5},{5,6},{6,7},{7,8},{8,9},{9,10},{10,1... | collective-permute-start | bytes 393224 | tf_op jit(solution)/shard_map/ppermute | solution.py:167
  295.3 7.1 %collective-permute-start.8 = (bf16[128,512]{1,0:T(8,128)(2,1)S(1)}, bf16[128,512]{1,0:T(8,128)(2,1)S(1)}, u32[]{:S(2)}, u32[]{:S(2)}) collective-permute-start(bf16[128,512]{1,0:T(8,128)(2,1)S(1)} %collective-permute-done.7), channel_id=1, source_target_pairs={{0,1},{1,2},{2,3},{3,4},{4,5},{5,6},{6,7},{7,8},{8,9},{9,10},{10,1... | collective-permute-start | bytes 393224 | tf_op jit(solution)/shard_map/ppermute | solution.py:167
  302.4 7.1 %collective-permute-start.9 = (bf16[128,512]{1,0:T(8,128)(2,1)S(1)}, bf16[128,512]{1,0:T(8,128)(2,1)S(1)}, u32[]{:S(2)}, u32[]{:S(2)}) collective-permute-start(bf16[128,512]{1,0:T(8,128)(2,1)S(1)} %collective-permute-done.8), channel_id=1, source_target_pairs={{0,1},{1,2},{2,3},{3,4},{4,5},{5,6},{6,7},{7,8},{8,9},{9,10},{10,1... | collective-permute-start | bytes 393224 | tf_op jit(solution)/shard_map/ppermute | solution.py:167
  309.5 7.1 %collective-permute-start.10 = (bf16[128,512]{1,0:T(8,128)(2,1)S(1)}, bf16[128,512]{1,0:T(8,128)(2,1)S(1)}, u32[]{:S(2)}, u32[]{:S(2)}) collective-permute-start(bf16[128,512]{1,0:T(8,128)(2,1)S(1)} %collective-permute-done.9), channel_id=1, source_target_pairs={{0,1},{1,2},{2,3},{3,4},{4,5},{5,6},{6,7},{7,8},{8,9},{9,10},{10,1... | collective-permute-start | bytes 393224 | tf_op jit(solution)/shard_map/ppermute | solution.py:167
  316.6 7.1 %collective-permute-start.11 = (bf16[128,512]{1,0:T(8,128)(2,1)S(1)}, bf16[128,512]{1,0:T(8,128)(2,1)S(1)}, u32[]{:S(2)}, u32[]{:S(2)}) collective-permute-start(bf16[128,512]{1,0:T(8,128)(2,1)S(1)} %collective-permute-done.10), channel_id=1, source_target_pairs={{0,1},{1,2},{2,3},{3,4},{4,5},{5,6},{6,7},{7,8},{8,9},{9,10},{10,1... | collective-permute-start | bytes 393224 | tf_op jit(solution)/shard_map/ppermute | solution.py:167
  323.7 7.1 %collective-permute-start.12 = (bf16[128,512]{1,0:T(8,128)(2,1)S(1)}, bf16[128,512]{1,0:T(8,128)(2,1)S(1)}, u32[]{:S(2)}, u32[]{:S(2)}) collective-permute-start(bf16[128,512]{1,0:T(8,128)(2,1)S(1)} %collective-permute-done.11), channel_id=1, source_target_pairs={{0,1},{1,2},{2,3},{3,4},{4,5},{5,6},{6,7},{7,8},{8,9},{9,10},{10,1... | collective-permute-start | bytes 393224 | tf_op jit(solution)/shard_map/ppermute | solution.py:167
  330.8 7.1 %collective-permute-start.13 = (bf16[128,512]{1,0:T(8,128)(2,1)S(1)}, bf16[128,512]{1,0:T(8,128)(2,1)S(1)}, u32[]{:S(2)}, u32[]{:S(2)}) collective-permute-start(bf16[128,512]{1,0:T(8,128)(2,1)S(1)} %collective-permute-done.12), channel_id=1, source_target_pairs={{0,1},{1,2},{2,3},{3,4},{4,5},{5,6},{6,7},{7,8},{8,9},{9,10},{10,1... | collective-permute-start | bytes 393224 | tf_op jit(solution)/shard_map/ppermute | solution.py:167
  337.9 7.1 %collective-permute-start.14 = (bf16[128,512]{1,0:T(8,128)(2,1)S(1)}, bf16[128,512]{1,0:T(8,128)(2,1)S(1)}, u32[]{:S(2)}, u32[]{:S(2)}) collective-permute-start(bf16[128,512]{1,0:T(8,128)(2,1)S(1)} %collective-permute-done.13), channel_id=1, source_target_pairs={{0,1},{1,2},{2,3},{3,4},{4,5},{5,6},{6,7},{7,8},{8,9},{9,10},{10,1... | collective-permute-start | bytes 393224 | tf_op jit(solution)/shard_map/ppermute | solution.py:167
  345.5 8.0 %slice-start = ((s8[14680064]{0:T(1024)(128)(4,1)}), s8[4194304]{0:T(1024)(128)(4,1)S(1)}, s32[]{:S(2)}) async-start(s8[14680064]{0:T(1024)(128)(4,1)} %bitcast.62), calls=%async_computation.5 | async-start | bytes 8388608
  345.8 7.7 %slice-start.1 = ((s8[14680064]{0:T(1024)(128)(4,1)}), s8[4194304]{0:T(1024)(128)(4,1)S(1)}, s32[]{:S(2)}) async-start(s8[14680064]{0:T(1024)(128)(4,1)} %bitcast.62), calls=%async_computation.6 | async-start | bytes 8388608
  345.8 8.6 %slice-start.2 = ((s8[14680064]{0:T(1024)(128)(4,1)}), s8[4194304]{0:T(1024)(128)(4,1)S(1)}, s32[]{:S(2)}) async-start(s8[14680064]{0:T(1024)(128)(4,1)} %bitcast.62), calls=%async_computation.7 | async-start | bytes 8388608
  345.8 9.2 %slice-start.3 = ((s8[14680064]{0:T(1024)(128)(4,1)}), s8[2097152]{0:T(1024)(128)(4,1)S(1)}, s32[]{:S(2)}) async-start(s8[14680064]{0:T(1024)(128)(4,1)} %bitcast.62), calls=%async_computation.8 | async-start | bytes 4194304
Sparse Core Ops, SparseCore 0:
  10.1 40.7 all-gather.2
  166.3 37.1 all-gather.4
